TPU v7x, 32 devices: a whole 2x2x4 slice. The times are simulated.
32 devices in a mesh: tm: 4 (over z), height: 8 (over y, x, core).
Axes of the slice: x: 2, y: 2, z: 4, core: 2. Of those that a mesh axis runs over, the one named last changes fastest.
Arguments:
- queries: bfloat16 [16, 16, 16, 2560], P('tm', 'height'), may hold values from -64 to 64
- keys: bfloat16 [16, 16, 16, 2560], P('tm', 'height'), may hold values from -64 to 64
- values: bfloat16 [16, 16, 16, 2560], P('tm', 'height'), may hold values from -6 to 6
- tile_mask: int32 [4, 8, 2, 18], P('tm', 'height'), may hold values 0 or 1
- sink_frame: int32 [1], replicated, may hold values from 0 to 15
Outputs:
- attended: bfloat16 [16, 16, 16, 2560], P('tm', 'height')
All inputs are finite; a program needn't handle non-finite values. No bound on the sum of `tile_mask` on one device may be relied on, other than what follows from the above.
Results may differ from a plain program's by a relative error of at most 0.0041.
Values may be sent and summed in bfloat16 or wider, within the bound.
No kernel may reach another device: no remote copies, remote signals or barrier semaphores. Data moves between devices by JAX's collectives and lax.ppermute only.
A program may use at most 128 MiB of HBM per device.

v0:
```python
import math
import jax
import jax.numpy as jnp
from jax import lax
from jax.sharding import PartitionSpec as P

H = 20
HD = 128
TF = 4
TC = 8
masked_score = -1e30


def from_behind(value, axis, steps):
    count = lax.axis_size(axis)
    first, last = (max(0, -steps), min(count, count - steps))
    return lax.ppermute(value, axis, [(source, source + steps) for source in range(first, last)])


def with_halo(cells, sides, width):
    for axis, dim in sides:
        count = lax.axis_size(axis)
        ends = count - 1
        head = lax.slice_in_dim(cells, 0, width, axis=dim)
        tail = lax.slice_in_dim(cells, cells.shape[dim] - width, cells.shape[dim], axis=dim)
        cells = jnp.concatenate(
            [
                lax.ppermute(tail, axis, [(i, (i + 1) % count) for i in range(ends)]),
                cells,
                lax.ppermute(head, axis, [((i + 1) % count, i) for i in range(ends)]),
            ],
            axis=dim,
        )
    return cells


def from_root(x, axis, root):
    mine = lax.axis_index(axis) == root
    return lax.psum(jnp.where(mine, x, jnp.zeros_like(x)), axis)


def near_allowed(tile_flags, time_base, band_index, band_total):
    q_tiles = tile_flags.shape[0]
    w_tiles = tile_flags.shape[1]
    q_time = jnp.arange(q_tiles)[:, None, None, None, None]
    q_width = jnp.arange(w_tiles)[None, :, None, None, None]
    slot = jnp.arange(2)[None, None, :, None, None]
    k_band = jnp.arange(3)[None, None, None, :, None] - 1
    width_slot = jnp.arange(3)[None, None, None, None, :]
    code_all = slot * 9 + (k_band + 1) * 3 + width_slot
    matches = code_all[..., None] == jnp.arange(tile_flags.shape[2])
    picked = jnp.sum(jnp.where(matches, tile_flags[:, :, None, None, None, :], 0), axis=-1) > 0
    itself = (slot == 1) & (k_band == 0) & (width_slot == 1)
    time_valid = time_base + q_time + slot - 1 >= 0
    band_now = band_index + k_band
    band_valid = (band_now >= 0) & (band_now < band_total)
    col_now = q_width + width_slot - 1
    col_valid = (col_now >= 0) & (col_now < w_tiles)
    return (picked | itself) & time_valid & band_valid & col_valid


def token_allowed(tiles_ok, row_count):
    q_tiles, w_tiles = (tiles_ok.shape[0], tiles_ok.shape[1])
    tile_tokens = TF * row_count * TC
    grid = tiles_ok[:, :, None, :, None, :, None, :, None]
    full = jnp.broadcast_to(grid, (q_tiles, w_tiles, tile_tokens, 2, TF, 3, row_count, 3, TC))
    return full.reshape(q_tiles, w_tiles, tile_tokens, 2 * TF * 3 * row_count * 3 * TC)


def shards(queries, keys, values, tile_mask, sink_frame):
    frames, row_count, col_count, features = queries.shape
    head_count = H
    scaling = 1.0 / math.sqrt(HD)
    local_tiles = frames // TF
    width_tiles = col_count // TC
    tile_tokens = TF * row_count * TC
    token_count = frames * row_count * col_count
    key_vals = jnp.stack((keys, values))
    prior_keys = from_behind(key_vals, "tm", 1)
    joined = jnp.concatenate((prior_keys, key_vals), axis=1)
    window = with_halo(joined, (("height", 2),), row_count)
    q_tiled = queries.reshape(local_tiles, TF, row_count, width_tiles, TC, head_count, HD)
    q_tiled = jnp.transpose(q_tiled, (0, 3, 1, 2, 4, 5, 6)).reshape(
        local_tiles, width_tiles, tile_tokens, head_count, HD
    )
    q_flat = q_tiled.reshape(token_count, head_count, HD)
    tiles_ok = near_allowed(
        tile_mask[:, 0],
        lax.axis_index("tm") * local_tiles,
        lax.axis_index("height"),
        lax.axis_size("height"),
    )
    allowed = token_allowed(tiles_ok, row_count)
    group_size = math.gcd(head_count, 4)
    group_count = head_count // group_size

    def head_step(step_no, running):
        run_max, run_sum, summed = running
        offset = step_no * group_size
        q_part = lax.dynamic_slice_in_dim(q_tiled, offset, group_size, 3)
        win_part = lax.dynamic_slice_in_dim(window, offset * HD, group_size * HD, 4)
        padded = jnp.pad(win_part, ((0, 0), (0, 0), (0, 0), (TC, TC), (0, 0)))
        tiled = padded.reshape(
            2, local_tiles + 1, TF, 3 * row_count, col_count + 2 * TC, group_size * HD
        )
        paired = jnp.stack((tiled[:, :-1], tiled[:, 1:]), axis=2)
        shifted = jnp.stack(
            [
                paired[:, :, :, :, :, shift_no * TC : shift_no * TC + col_count]
                for shift_no in range(3)
            ],
            axis=5,
        )
        shifted = shifted.reshape(
            2, local_tiles, 2, TF, 3, row_count, 3, width_tiles, TC, group_size, HD
        )
        shifted = jnp.transpose(shifted, (0, 1, 7, 2, 3, 4, 5, 6, 8, 9, 10))
        shifted = shifted.reshape(2, local_tiles, width_tiles, -1, group_size, HD)
        scores = (
            jnp.einsum("tcqhd,tckhd->tchqk", q_part, shifted[0], preferred_element_type=jnp.float32)
            * scaling
        )
        scores = jnp.where(allowed[:, :, None], scores, masked_score)
        row_max = jnp.max(scores, axis=-1)
        weights = jnp.exp(scores - row_max[..., None]).astype(jnp.bfloat16)
        row_sum = jnp.sum(weights, axis=-1, dtype=jnp.float32)
        partial_out = jnp.einsum(
            "tchqk,tckhd->tcqhd", weights, shifted[1], preferred_element_type=jnp.float32
        )
        row_max = jnp.transpose(row_max, (2, 0, 1, 3)).reshape(group_size, token_count)
        row_sum = jnp.transpose(row_sum, (2, 0, 1, 3)).reshape(group_size, token_count)
        partial_out = partial_out.reshape(token_count, group_size, HD)
        run_max = lax.dynamic_update_slice_in_dim(run_max, row_max, offset, 0)
        run_sum = lax.dynamic_update_slice_in_dim(run_sum, row_sum, offset, 0)
        summed = lax.dynamic_update_slice_in_dim(summed, partial_out, offset, 1)
        return (run_max, run_sum, summed)

    window_init = (
        jnp.zeros((head_count, token_count), jnp.float32),
        jnp.zeros((head_count, token_count), jnp.float32),
        jnp.zeros((token_count, head_count, HD), jnp.float32),
    )
    win_max, win_sum, win_out = lax.fori_loop(0, group_count, head_step, window_init)
    sink_init = (
        jnp.full((head_count, token_count), masked_score, jnp.float32),
        jnp.zeros((head_count, token_count), jnp.float32),
        jnp.zeros((token_count, head_count, HD), jnp.float32),
    )
    owner_index = sink_frame[0] // frames
    local_frame = sink_frame[0] % frames
    sink_piece = lax.dynamic_slice_in_dim(key_vals, local_frame, 1, 1)[:, 0]
    sliced = from_root(sink_piece, "tm", owner_index)
    shard_rows = lax.all_gather(sliced, "height", axis=1, tiled=True)
    band_total = shard_rows.shape[1] // row_count

    def band_step(step_no, state):
        run_max, run_sum, summed = state
        block_rows = lax.dynamic_slice_in_dim(shard_rows, step_no * row_count, row_count, 1)
        key_block = block_rows[0].reshape(row_count * col_count, head_count, HD)
        val_block = block_rows[1].reshape(row_count * col_count, head_count, HD)
        scores = (
            jnp.einsum("qhd,khd->hqk", q_flat, key_block, preferred_element_type=jnp.float32)
            * scaling
        )
        row_max = jnp.max(scores, axis=-1)
        weights = jnp.exp(scores - row_max[..., None]).astype(jnp.bfloat16)
        row_sum = jnp.sum(weights, axis=-1, dtype=jnp.float32)
        added = jnp.einsum("hqk,khd->qhd", weights, val_block, preferred_element_type=jnp.float32)
        new_max = jnp.maximum(run_max, row_max)
        keep_old = jnp.exp(run_max - new_max)
        factor = jnp.exp(row_max - new_max)
        run_sum = run_sum * keep_old + row_sum * factor
        summed = summed * keep_old.T[..., None] + added * factor.T[..., None]
        return (new_max, run_sum, summed)

    sink_max, sink_sum, sink_out = lax.fori_loop(0, band_total, band_step, sink_init)
    top_score = jnp.maximum(win_max, sink_max)
    win_factor = jnp.exp(win_max - top_score)
    sink_factor = jnp.exp(sink_max - top_score)
    denominator = win_factor * win_sum + sink_factor * sink_sum
    numerator = win_out * win_factor.T[..., None] + sink_out * sink_factor.T[..., None]
    result = (numerator / denominator.T[..., None]).astype(jnp.bfloat16)
    result = result.reshape(local_tiles, width_tiles, TF, row_count, TC, features)
    result = jnp.transpose(result, (0, 2, 3, 1, 4, 5))
    return result.reshape(frames, row_count, col_count, features)


def solution(mesh):
    return jax.shard_map(
        shards,
        mesh=mesh,
        in_specs=(
            P("tm", "height", None, None),
            P("tm", "height", None, None),
            P("tm", "height", None, None),
            P("tm", "height", None, None),
            P(),
        ),
        out_specs=P("tm", "height", None, None),
        check_vma=False,
    )
```

profile of v0, /device:TPU:1, one launch (start us, length us, event | category | flops | bytes accessed | tf_op | source)
XLA Modules:
  0.0 239.6 jit_solution(7108686175418753605)
XLA Ops:
  6.5 2.6 %pad_maximum_fusion.2 = bf16[2,4,2,16,2560]{4,3,2,0,1:T(8,128)(2,1)} fusion(bf16[1,4,2,16,2560]{4,3,2,0,1:T(8,128)(2,1)} %bitcast.136, bf16[1,4,2,16,2560]{4,3,2,0,1:T(8,128)(2,1)} %bitcast.132), kind=kLoop, calls=%fused_computation.45 | loop fusion | flops 655360 | bytes 2621440 | tf_op jit(solution)/shard_map/stack | solution.py:78
  9.2 4.1 %collective-permute-start = (bf16[2,4,2,16,2560]{4,3,2,0,1:T(8,128)(2,1)}, bf16[2,4,2,16,2560]{4,3,2,0,1:T(8,128)(2,1)S(1)}, u32[]{:S(2)}, u32[]{:S(2)}) collective-permute-start(bf16[2,4,2,16,2560]{4,3,2,0,1:T(8,128)(2,1)} %pad_maximum_fusion.2), channel_id=1, source_target_pairs={{0,8},{8,16},{16,24},{1,9},{9,17},{17,25},{2,10},{10,18},{18,26},{... | collective-permute-start | bytes 3932168 | tf_op jit(solution)/shard_map/ppermute | solution.py:17
  14.0 27.0 %collective-permute-done = bf16[2,4,2,16,2560]{4,3,2,0,1:T(8,128)(2,1)S(1)} collective-permute-done((bf16[2,4,2,16,2560]{4,3,2,0,1:T(8,128)(2,1)}, bf16[2,4,2,16,2560]{4,3,2,0,1:T(8,128)(2,1)S(1)}, u32[]{:S(2)}, u32[]{:S(2)}) %collective-permute-start) | collective-permute-done | bytes 1310752 | tf_op jit(solution)/shard_map/ppermute | solution.py:17
  41.0 1.8 maximum_maximum_fusion
  42.7 4.5 %collective-permute-start.1 = (bf16[2,8,2,16,2560]{4,3,2,0,1:T(8,128)(2,1)}, bf16[2,8,2,16,2560]{4,3,2,0,1:T(8,128)(2,1)}, u32[]{:S(2)}, u32[]{:S(2)}) collective-permute-start(bf16[2,8,2,16,2560]{4,3,2,0,1:T(8,128)(2,1)} %maximum_maximum_fusion), channel_id=1, source_target_pairs={{0,1},{1,2},{2,3},{3,4},{4,5},{5,6},{6,7},{8,9},{9,10},{10,11},{11... | collective-permute-start | bytes 7864328 | tf_op jit(solution)/shard_map/ppermute | solution.py:28
  47.2 1.9 collective-permute-start.2
  53.2 33.5 %all-reduce.3.cloned.1.call-done = bf16[2,2,16,2560]{3,2,1,0:T(8,128)(2,1)} async-done(((bf16[2,2,16,2560]{3,2,1,0:T(8,128)(2,1)}), bf16[2,2,16,2560]{3,2,1,0:T(8,128)(2,1)}) %all-reduce.3.cloned.1.call-update) | async-done | bytes 327696 | tf_op jit(solution)/shard_map/psum | solution.py:39
  86.7 22.7 %collective-permute-done.2 = bf16[2,8,2,16,2560]{4,3,2,0,1:T(8,128)(2,1)} collective-permute-done((bf16[2,8,2,16,2560]{4,3,2,0,1:T(8,128)(2,1)}, bf16[2,8,2,16,2560]{4,3,2,0,1:T(8,128)(2,1)}, u32[]{:S(2)}, u32[]{:S(2)}) %collective-permute-start.2) | collective-permute-done | bytes 2621472 | tf_op jit(solution)/shard_map/ppermute | solution.py:30
  109.4 6.5 %pad_maximum_fusion.1 = bf16[2,8,6,16,2560]{4,3,2,0,1:T(8,128)(2,1)} fusion(bf16[2,8,2,16,2560]{4,3,2,0,1:T(8,128)(2,1)} %collective-permute-done.2, bf16[1,4,2,16,2560]{4,3,2,0,1:T(8,128)(2,1)S(1)} %bitcast.139, bf16[1,4,2,16,2560]{4,3,2,0,1:T(8,128)(2,1)S(1)} %bitcast.135, bf16[2,4,2,16,2560]{4,3,2,0,1:T(8,128)(2,1)S(1)} %collective-permute-done, ...), kind=kLoop, calls=%fused_computation.42 | loop fusion | flops 15728640 | bytes 15728640 | tf_op jit(solution)/shard_map/concatenate | solution.py:26
  117.1 74.7 %while.38 = (s32[]{:T(128)}, f32[20,128]{1,0:T(8,128)S(1)}, f32[20,128]{1,0:T(8,128)S(1)}, f32[128,20,128]{0,2,1:T(8,128)}, bf16[1,2,64,20,128]{4,2,3,1,0:T(8,12...) while((s32[]{:T(128)}, f32[20,128]{1,0:T(8,128)S(1)}, ...), condition=%wide.region_4.5_spmd.clone, body=%wide.region_1.4_spmd.clone.sunk | while | flops 321453056 | bytes 86737208 | solution.py:143
  117.1 1.5 constant_dynamic-slice_fusion.5
  121.1 2.5 %fusion.46 = (bf16[1,1,2,2,4,3,2,3,8,4,128]{10,8,9,2,7,6,5,4,3,1,0:T(8,128)(2,1)}, bf16[1,1,2,2,4,3,2,3,8,4,128]{10,8,9,2,7,6,5,4,3,1,0:T(8,128)(2,1)S(1)}) fusion(bf16[2,1,2,2,4,3,2,3,8,4,128]{10,8,9,2,7,6,5,4,3,1,0:T(8,128)(2,1)S(1)} %maximum_bitcast_fusion.2), kind=kLoop, calls=%fused_computation.76.clone.1 | loop fusion | bytes 9437184 | tf_op jit(solution)/shard_map/while/body/eval_jaxpr/slice | solution.py:128
  123.6 2.0 copy.127
  126.2 3.0 %fusion.47 = (f32[2,4,64]{2,1,0:T(4,128)S(1)}, f32[2,4,64,1152]{3,2,1,0:T(8,128)S(1)}) fusion(bf16[2,1152,4,128]{3,1,2,0:T(8,128)(2,1)} %bitcast.124, bf16[1,2,64,20,128]{4,2,3,1,0:T(8,128)(2,1)} %get-tuple-element.616, s32[]{:T(128)S(6)} %select_n.100, pred[2,64,1152]{2,1,0:T(8,128)(4,1)S(1)} %copy.128), kind=kOutput, calls=%fused_computation.77.clone.1 | convolution fusion | flops 152763904 | bytes 4999172 | tf_op jit(solution)/shard_map/while/body/eval_jaxpr/tcqhd,tckhd->tchqk/dot_general | solution.py:120
  136.0 2.5 %fusion.46 = (bf16[1,1,2,2,4,3,2,3,8,4,128]{10,8,9,2,7,6,5,4,3,1,0:T(8,128)(2,1)}, bf16[1,1,2,2,4,3,2,3,8,4,128]{10,8,9,2,7,6,5,4,3,1,0:T(8,128)(2,1)S(1)}) fusion(bf16[2,1,2,2,4,3,2,3,8,4,128]{10,8,9,2,7,6,5,4,3,1,0:T(8,128)(2,1)S(1)} %maximum_bitcast_fusion.2), kind=kLoop, calls=%fused_computation.76.clone.1 | loop fusion | bytes 9437184 | tf_op jit(solution)/shard_map/while/body/eval_jaxpr/slice | solution.py:128
  138.5 2.0 copy.127
  141.1 3.0 %fusion.47 = (f32[2,4,64]{2,1,0:T(4,128)S(1)}, f32[2,4,64,1152]{3,2,1,0:T(8,128)S(1)}) fusion(bf16[2,1152,4,128]{3,1,2,0:T(8,128)(2,1)} %bitcast.124, bf16[1,2,64,20,128]{4,2,3,1,0:T(8,128)(2,1)} %get-tuple-element.616, s32[]{:T(128)S(6)} %select_n.100, pred[2,64,1152]{2,1,0:T(8,128)(4,1)S(1)} %copy.128), kind=kOutput, calls=%fused_computation.77.clone.1 | convolution fusion | flops 152763904 | bytes 4999172 | tf_op jit(solution)/shard_map/while/body/eval_jaxpr/tcqhd,tckhd->tchqk/dot_general | solution.py:120
  150.9 2.5 %fusion.46 = (bf16[1,1,2,2,4,3,2,3,8,4,128]{10,8,9,2,7,6,5,4,3,1,0:T(8,128)(2,1)}, bf16[1,1,2,2,4,3,2,3,8,4,128]{10,8,9,2,7,6,5,4,3,1,0:T(8,128)(2,1)S(1)}) fusion(bf16[2,1,2,2,4,3,2,3,8,4,128]{10,8,9,2,7,6,5,4,3,1,0:T(8,128)(2,1)S(1)} %maximum_bitcast_fusion.2), kind=kLoop, calls=%fused_computation.76.clone.1 | loop fusion | bytes 9437184 | tf_op jit(solution)/shard_map/while/body/eval_jaxpr/slice | solution.py:128
  153.5 2.0 copy.127
  156.0 3.0 %fusion.47 = (f32[2,4,64]{2,1,0:T(4,128)S(1)}, f32[2,4,64,1152]{3,2,1,0:T(8,128)S(1)}) fusion(bf16[2,1152,4,128]{3,1,2,0:T(8,128)(2,1)} %bitcast.124, bf16[1,2,64,20,128]{4,2,3,1,0:T(8,128)(2,1)} %get-tuple-element.616, s32[]{:T(128)S(6)} %select_n.100, pred[2,64,1152]{2,1,0:T(8,128)(4,1)S(1)} %copy.128), kind=kOutput, calls=%fused_computation.77.clone.1 | convolution fusion | flops 152763904 | bytes 4999172 | tf_op jit(solution)/shard_map/while/body/eval_jaxpr/tcqhd,tckhd->tchqk/dot_general | solution.py:120
  165.9 2.5 %fusion.46 = (bf16[1,1,2,2,4,3,2,3,8,4,128]{10,8,9,2,7,6,5,4,3,1,0:T(8,128)(2,1)}, bf16[1,1,2,2,4,3,2,3,8,4,128]{10,8,9,2,7,6,5,4,3,1,0:T(8,128)(2,1)S(1)}) fusion(bf16[2,1,2,2,4,3,2,3,8,4,128]{10,8,9,2,7,6,5,4,3,1,0:T(8,128)(2,1)S(1)} %maximum_bitcast_fusion.2), kind=kLoop, calls=%fused_computation.76.clone.1 | loop fusion | bytes 9437184 | tf_op jit(solution)/shard_map/while/body/eval_jaxpr/slice | solution.py:128
  168.4 2.0 copy.127
  171.0 3.0 %fusion.47 = (f32[2,4,64]{2,1,0:T(4,128)S(1)}, f32[2,4,64,1152]{3,2,1,0:T(8,128)S(1)}) fusion(bf16[2,1152,4,128]{3,1,2,0:T(8,128)(2,1)} %bitcast.124, bf16[1,2,64,20,128]{4,2,3,1,0:T(8,128)(2,1)} %get-tuple-element.616, s32[]{:T(128)S(6)} %select_n.100, pred[2,64,1152]{2,1,0:T(8,128)(4,1)S(1)} %copy.128), kind=kOutput, calls=%fused_computation.77.clone.1 | convolution fusion | flops 152763904 | bytes 4999172 | tf_op jit(solution)/shard_map/while/body/eval_jaxpr/tcqhd,tckhd->tchqk/dot_general | solution.py:120
  180.8 2.5 %fusion.46 = (bf16[1,1,2,2,4,3,2,3,8,4,128]{10,8,9,2,7,6,5,4,3,1,0:T(8,128)(2,1)}, bf16[1,1,2,2,4,3,2,3,8,4,128]{10,8,9,2,7,6,5,4,3,1,0:T(8,128)(2,1)S(1)}) fusion(bf16[2,1,2,2,4,3,2,3,8,4,128]{10,8,9,2,7,6,5,4,3,1,0:T(8,128)(2,1)S(1)} %maximum_bitcast_fusion.2), kind=kLoop, calls=%fused_computation.76.clone.1 | loop fusion | bytes 9437184 | tf_op jit(solution)/shard_map/while/body/eval_jaxpr/slice | solution.py:128
  183.3 2.0 copy.127
  185.9 3.0 %fusion.47 = (f32[2,4,64]{2,1,0:T(4,128)S(1)}, f32[2,4,64,1152]{3,2,1,0:T(8,128)S(1)}) fusion(bf16[2,1152,4,128]{3,1,2,0:T(8,128)(2,1)} %bitcast.124, bf16[1,2,64,20,128]{4,2,3,1,0:T(8,128)(2,1)} %get-tuple-element.616, s32[]{:T(128)S(6)} %select_n.100, pred[2,64,1152]{2,1,0:T(8,128)(4,1)S(1)} %copy.128), kind=kOutput, calls=%fused_computation.77.clone.1 | convolution fusion | flops 152763904 | bytes 4999172 | tf_op jit(solution)/shard_map/while/body/eval_jaxpr/tcqhd,tckhd->tchqk/dot_general | solution.py:120
  191.8 37.5 %while.39 = (s32[]{:T(128)}, f32[20,128]{1,0:T(8,128)S(1)}, f32[20,128]{1,0:T(8,128)S(1)}, f32[128,20,128]{0,2,1:T(8,128)}, bf16[2,16,16,2560]{3,2,1,0:T(8,128)(...) while((s32[]{:T(128)}, f32[20,128]{1,0:T(8,128)S(1)}, ...), condition=%wide.region_9.10_spmd.clone, body=%wide.region_6.9_spmd.clone.sunk | while | flops 43929608 | bytes 16578803 | solution.py:176
  193.1 1.5 fusion.50
  197.8 1.5 fusion.50
  202.5 1.5 fusion.50
  207.2 1.5 fusion.50
  229.3 1.7 divide_convert_fusion
  (265 shorter events, 72.3 us)
Async XLA Ops:
  6.5 44.5 %copy-start = (bf16[4,2,16,2560]{3,2,1,0:T(8,128)(2,1)S(1)}, bf16[4,2,16,2560]{3,2,1,0:T(8,128)(2,1)}, u32[]{:S(2)}) copy-start(bf16[4,2,16,2560]{3,2,1,0:T(8,128)(2,1)} %param.9) | copy-start | bytes 1966084
  6.5 34.4 %copy-start.5 = (bf16[4,2,16,2560]{3,2,1,0:T(8,128)(2,1)S(1)}, bf16[4,2,16,2560]{3,2,1,0:T(8,128)(2,1)}, u32[]{:S(2)}) copy-start(bf16[4,2,16,2560]{3,2,1,0:T(8,128)(2,1)} %param.10) | copy-start | bytes 1966084
  6.5 34.4 %copy-start.6 = (bf16[4,2,16,2560]{3,2,1,0:T(8,128)(2,1)S(1)}, bf16[4,2,16,2560]{3,2,1,0:T(8,128)(2,1)}, u32[]{:S(2)}) copy-start(bf16[4,2,16,2560]{3,2,1,0:T(8,128)(2,1)} %param.11) | copy-start | bytes 1966084
  6.5 80.1 %all-reduce.3.cloned.1.call-start = ((), (), s32[]{:S(2)}) async-start(), calls=%async_computation | async-start | bytes 655360 | tf_op jit(solution)/shard_map/psum | solution.py:39
  9.2 31.8 %collective-permute-start = (bf16[2,4,2,16,2560]{4,3,2,0,1:T(8,128)(2,1)}, bf16[2,4,2,16,2560]{4,3,2,0,1:T(8,128)(2,1)S(1)}, u32[]{:S(2)}, u32[]{:S(2)}) collective-permute-start(bf16[2,4,2,16,2560]{4,3,2,0,1:T(8,128)(2,1)} %pad_maximum_fusion.2), channel_id=1, source_target_pairs={{0,8},{8,16},{16,24},{1,9},{9,17},{17,25},{2,10},{10,18},{18,26},{... | collective-permute-start | bytes 3932168 | tf_op jit(solution)/shard_map/ppermute | solution.py:17
  14.0 36.3 %copy-start.8 = (s32[1,1,2,18]{3,2,1,0:T(2,128)S(1)}, s32[1,1,2,18]{3,2,1,0:T(2,128)}, u32[]{:S(2)}) copy-start(s32[1,1,2,18]{3,2,1,0:T(2,128)} %param.12) | copy-start | bytes 436
  42.7 44.0 %collective-permute-start.1 = (bf16[2,8,2,16,2560]{4,3,2,0,1:T(8,128)(2,1)}, bf16[2,8,2,16,2560]{4,3,2,0,1:T(8,128)(2,1)}, u32[]{:S(2)}, u32[]{:S(2)}) collective-permute-start(bf16[2,8,2,16,2560]{4,3,2,0,1:T(8,128)(2,1)} %maximum_maximum_fusion), channel_id=1, source_target_pairs={{0,1},{1,2},{2,3},{3,4},{4,5},{5,6},{6,7},{8,9},{9,10},{10,11},{11... | collective-permute-start | bytes 7864328 | tf_op jit(solution)/shard_map/ppermute | solution.py:28
  47.2 62.1 %collective-permute-start.2 = (bf16[2,8,2,16,2560]{4,3,2,0,1:T(8,128)(2,1)}, bf16[2,8,2,16,2560]{4,3,2,0,1:T(8,128)(2,1)}, u32[]{:S(2)}, u32[]{:S(2)}) collective-permute-start(bf16[2,8,2,16,2560]{4,3,2,0,1:T(8,128)(2,1)} %maximum_maximum_fusion), channel_id=1, source_target_pairs={{1,0},{2,1},{3,2},{4,3},{5,4},{6,5},{7,6},{9,8},{10,9},{11,10},{12... | collective-permute-start | bytes 7864328 | tf_op jit(solution)/shard_map/ppermute | solution.py:30
  50.0 141.8 %all-gather.2.cloned.1.call-start = ((), (), s32[]{:S(2)}) async-start(), calls=%async_computation.1 | async-start | bytes 2949120 | tf_op jit(solution)/shard_map/all_gather | solution.py:153
  126.1 3.0 %copy-start.2 = (bf16[1,1,2,2,4,3,2,3,8,4,128]{10,8,9,2,7,6,5,4,3,1,0:T(8,128)(2,1)S(1)}, bf16[1,1,2,2,4,3,2,3,8,4,128]{10,8,9,2,7,6,5,4,3,1,0:T(8,128)(2,1)}, u32[]{:S(2)}) copy-start(bf16[1,1,2,2,4,3,2,3,8,4,128]{10,8,9,2,7,6,5,4,3,1,0:T(8,128)(2,1)} %get-tuple-element.536) | copy-start | bytes 7077892 | tf_op jit(solution)/shard_map/while
  141.1 3.0 %copy-start.2 = (bf16[1,1,2,2,4,3,2,3,8,4,128]{10,8,9,2,7,6,5,4,3,1,0:T(8,128)(2,1)S(1)}, bf16[1,1,2,2,4,3,2,3,8,4,128]{10,8,9,2,7,6,5,4,3,1,0:T(8,128)(2,1)}, u32[]{:S(2)}) copy-start(bf16[1,1,2,2,4,3,2,3,8,4,128]{10,8,9,2,7,6,5,4,3,1,0:T(8,128)(2,1)} %get-tuple-element.536) | copy-start | bytes 7077892 | tf_op jit(solution)/shard_map/while
  156.0 3.0 %copy-start.2 = (bf16[1,1,2,2,4,3,2,3,8,4,128]{10,8,9,2,7,6,5,4,3,1,0:T(8,128)(2,1)S(1)}, bf16[1,1,2,2,4,3,2,3,8,4,128]{10,8,9,2,7,6,5,4,3,1,0:T(8,128)(2,1)}, u32[]{:S(2)}) copy-start(bf16[1,1,2,2,4,3,2,3,8,4,128]{10,8,9,2,7,6,5,4,3,1,0:T(8,128)(2,1)} %get-tuple-element.536) | copy-start | bytes 7077892 | tf_op jit(solution)/shard_map/while
  171.0 3.0 %copy-start.2 = (bf16[1,1,2,2,4,3,2,3,8,4,128]{10,8,9,2,7,6,5,4,3,1,0:T(8,128)(2,1)S(1)}, bf16[1,1,2,2,4,3,2,3,8,4,128]{10,8,9,2,7,6,5,4,3,1,0:T(8,128)(2,1)}, u32[]{:S(2)}) copy-start(bf16[1,1,2,2,4,3,2,3,8,4,128]{10,8,9,2,7,6,5,4,3,1,0:T(8,128)(2,1)} %get-tuple-element.536) | copy-start | bytes 7077892 | tf_op jit(solution)/shard_map/while
  185.9 3.0 %copy-start.2 = (bf16[1,1,2,2,4,3,2,3,8,4,128]{10,8,9,2,7,6,5,4,3,1,0:T(8,128)(2,1)S(1)}, bf16[1,1,2,2,4,3,2,3,8,4,128]{10,8,9,2,7,6,5,4,3,1,0:T(8,128)(2,1)}, u32[]{:S(2)}) copy-start(bf16[1,1,2,2,4,3,2,3,8,4,128]{10,8,9,2,7,6,5,4,3,1,0:T(8,128)(2,1)} %get-tuple-element.536) | copy-start | bytes 7077892 | tf_op jit(solution)/shard_map/while
  191.8 37.5 %copy-start.7 = (f32[128,20,128]{0,2,1:T(8,128)S(1)}, f32[128,20,128]{0,2,1:T(8,128)}, u32[]{:S(2)}) copy-start(f32[128,20,128]{0,2,1:T(8,128)} %get-tuple-element.295) | copy-start | bytes 3932164
  191.8 3.1 %copy-start.3 = (f32[128,20,128]{0,2,1:T(8,128)S(1)}, f32[128,20,128]{0,2,1:T(8,128)}, u32[]{:S(2)}) copy-start(f32[128,20,128]{0,2,1:T(8,128)} %get-tuple-element.565) | copy-start | bytes 3932164 | tf_op jit(solution)/shard_map/while
  195.5 1.1 copy-start.4
  196.6 3.0 %copy-start.3 = (f32[128,20,128]{0,2,1:T(8,128)S(1)}, f32[128,20,128]{0,2,1:T(8,128)}, u32[]{:S(2)}) copy-start(f32[128,20,128]{0,2,1:T(8,128)} %get-tuple-element.565) | copy-start | bytes 3932164 | tf_op jit(solution)/shard_map/while
  200.2 1.1 copy-start.4
  201.2 3.0 %copy-start.3 = (f32[128,20,128]{0,2,1:T(8,128)S(1)}, f32[128,20,128]{0,2,1:T(8,128)}, u32[]{:S(2)}) copy-start(f32[128,20,128]{0,2,1:T(8,128)} %get-tuple-element.565) | copy-start | bytes 3932164 | tf_op jit(solution)/shard_map/while
  204.8 1.1 copy-start.4
  205.9 3.0 %copy-start.3 = (f32[128,20,128]{0,2,1:T(8,128)S(1)}, f32[128,20,128]{0,2,1:T(8,128)}, u32[]{:S(2)}) copy-start(f32[128,20,128]{0,2,1:T(8,128)} %get-tuple-element.565) | copy-start | bytes 3932164 | tf_op jit(solution)/shard_map/while
  209.5 1.1 copy-start.4
  210.6 3.0 %copy-start.3 = (f32[128,20,128]{0,2,1:T(8,128)S(1)}, f32[128,20,128]{0,2,1:T(8,128)}, u32[]{:S(2)}) copy-start(f32[128,20,128]{0,2,1:T(8,128)} %get-tuple-element.565) | copy-start | bytes 3932164 | tf_op jit(solution)/shard_map/while
  214.2 1.1 copy-start.4
  215.3 3.0 %copy-start.3 = (f32[128,20,128]{0,2,1:T(8,128)S(1)}, f32[128,20,128]{0,2,1:T(8,128)}, u32[]{:S(2)}) copy-start(f32[128,20,128]{0,2,1:T(8,128)} %get-tuple-element.565) | copy-start | bytes 3932164 | tf_op jit(solution)/shard_map/while
  218.9 1.1 copy-start.4
  219.9 3.0 %copy-start.3 = (f32[128,20,128]{0,2,1:T(8,128)S(1)}, f32[128,20,128]{0,2,1:T(8,128)}, u32[]{:S(2)}) copy-start(f32[128,20,128]{0,2,1:T(8,128)} %get-tuple-element.565) | copy-start | bytes 3932164 | tf_op jit(solution)/shard_map/while
  223.5 1.1 copy-start.4
  224.6 3.0 %copy-start.3 = (f32[128,20,128]{0,2,1:T(8,128)S(1)}, f32[128,20,128]{0,2,1:T(8,128)}, u32[]{:S(2)}) copy-start(f32[128,20,128]{0,2,1:T(8,128)} %get-tuple-element.565) | copy-start | bytes 3932164 | tf_op jit(solution)/shard_map/while
  228.2 1.1 copy-start.4
  229.3 3.4 %copy-start.1 = (bf16[4,2,16,2560]{3,2,1,0:T(8,128)(2,1)S(1)}, bf16[4,2,16,2560]{3,2,1,0:T(8,128)(2,1)}, u32[]{:S(2)}) copy-start(bf16[4,2,16,2560]{3,2,1,0:T(8,128)(2,1)} %param.9) | copy-start | bytes 1966084
Sparse Core Ops, SparseCore 0:
  50.1 36.5 all-reduce.2
  88.5 35.1 all-gather.1
where the time goes:
time: 240 us
  waiting for transfers between devices  83.2 us (35%)
  local copies, waits for them, and re-layouts  72.7 us (30%)
  matrix products  35 us (15%)
  other arithmetic  22.5 us (9%)
  between operations  14.2 us (6%)
  starting transfers between devices  10.6 us (4%)
    psum x1, waiting for transfers between devices, from_root(): return lax.psum(jnp.where(mine, x, jnp.zeros_like(x)), axis)  33.5 us
    ppermute x1, waiting for transfers between devices, from_behind(): lax.ppermute(value, axis, [(source, source + steps) for source in range(f...  27 us
    ppermute x1, waiting for transfers between devices, with_halo(): lax.ppermute(head, axis, [((i + 1) % count, i) for i in range(ends)])  22.7 us
    slice x10, local copies, waits for them, and re-layouts, head_step(): shifted[1]  15.8 us
    dot_general x5, matrix products, head_step(): jnp.einsum('tcqhd,tckhd->tchqk', q_part, shifted[0], preferred_element_ty...  14.9 us
    dot_general x8, matrix products, band_step(): jnp.einsum('qhd,khd->hqk', q_flat, key_block, preferred_element_type=jnp....  12.4 us
    slice x5, local copies, waits for them, and re-layouts, head_step(): shifted[0]  10 us
    slice x8, local copies, waits for them, and re-layouts, band_step(): val_block = block_rows[1].reshape(row_count * col_count, head_count, HD)  9.01 us
  transfers between devices with their start and end apart: 5, of which 3 were waited for; matrix products, arithmetic and copies ran while one was open for 36% of the time, Pallas kernels for 0%

commit v1 on v0

--- a/solution.py
+++ b/solution.py
@@ -36,7 +36,7 @@
 
 def from_root(x, axis, root):
     mine = lax.axis_index(axis) == root
-    return lax.psum(jnp.where(mine, x, jnp.zeros_like(x)), axis)
+    return jnp.sum(lax.all_gather(jnp.where(mine, x, jnp.zeros_like(x)), axis), axis=0)
 
 
 def near_allowed(tile_flags, time_base, band_index, band_total):

time: 240 us -> 267 us (1.11)
  waiting for transfers between devices: 83.2 us -> 105 us
    psum x1 -> x0, waiting for transfers between devices: 33.5 us -> none  [from_root(): return lax.psum(jnp.where(mine, x, jnp.zeros_like(x)), axis)]
    ppermute x1, waiting for transfers between devices: 0.01 us -> 25 us  [with_halo(): lax.ppermute(tail, axis, [(i, (i + 1) % count) for i in range(ends)])]
    ppermute x1, waiting for transfers between devices: 27 us -> 43.2 us  [from_behind(): lax.ppermute(value, axis, [(source, source + steps) for source in range(f...]
    ppermute x1, waiting for transfers between devices: 22.7 us -> 36.8 us  [with_halo(): lax.ppermute(head, axis, [((i + 1) % count, i) for i in range(ends)])]
    dynamic_slice x10 -> x5, local copies, waits for them, and re-layouts: 8.49 us -> 7.66 us  [head_step(): win_part = lax.dynamic_slice_in_dim(window, offset * HD, group_size * HD, 4)]
  transfers between devices with their start and end apart: 5 -> 5, of which waited for: 3 -> 3; matrix products, arithmetic and copies ran while one was open for 36% -> 33% of each run, Pallas kernels for 0% -> 0%
where the time goes in v1:
time: 267 us; the launch traced here: 265 us
  waiting for transfers between devices  105 us (39%)
  local copies, waits for them, and re-layouts  71.9 us (27%)
  matrix products  35 us (13%)
  other arithmetic  24.6 us (9%)
  between operations  14.3 us (5%)
  starting transfers between devices  12.6 us (5%)
    ppermute x1, waiting for transfers between devices, from_behind(): lax.ppermute(value, axis, [(source, source + steps) for source in range(f...  43.2 us
    ppermute x1, waiting for transfers between devices, with_halo(): lax.ppermute(head, axis, [((i + 1) % count, i) for i in range(ends)])  36.8 us
    ppermute x1, waiting for transfers between devices, with_halo(): lax.ppermute(tail, axis, [(i, (i + 1) % count) for i in range(ends)])  25 us
    slice x10, local copies, waits for them, and re-layouts, head_step(): shifted[1]  15.8 us
    dot_general x5, matrix products, head_step(): jnp.einsum('tcqhd,tckhd->tchqk', q_part, shifted[0], preferred_element_ty...  14.9 us
    dot_general x8, matrix products, band_step(): jnp.einsum('qhd,khd->hqk', q_flat, key_block, preferred_element_type=jnp....  12.4 us
    slice x5, local copies, waits for them, and re-layouts, head_step(): shifted[0]  10 us
    slice x8, local copies, waits for them, and re-layouts, band_step(): val_block = block_rows[1].reshape(row_count * col_count, head_count, HD)  9.01 us
  transfers between devices with their start and end apart: 5, of which 3 were waited for; matrix products, arithmetic and copies ran while one was open for 33% of the time, Pallas kernels for 0%

profile of v1, /device:TPU:1, one launch (start us, length us, event | category | flops | bytes accessed | tf_op | source)
XLA Modules:
  0.0 264.7 jit_solution(10323690618011730060)
XLA Ops:
  6.5 2.6 pad_maximum_fusion.2
  9.2 4.1 %collective-permute-start = (bf16[2,4,2,16,2560]{4,3,2,1,0:T(8,128)(2,1)}, bf16[2,4,2,16,2560]{4,3,2,1,0:T(8,128)(2,1)S(1)}, u32[]{:S(2)}, u32[]{:S(2)}) collective-permute-start(bf16[2,4,2,16,2560]{4,3,2,1,0:T(8,128)(2,1)} %pad_maximum_fusion.2), channel_id=1, source_target_pairs={{0,8},{8,16},{16,24},{1,9},{9,17},{17,25},{2,10},{10,18},{18,26},{... | collective-permute-start | bytes 3932168 | tf_op jit(solution)/shard_map/ppermute | solution.py:17
  14.8 43.2 %collective-permute-done = bf16[2,4,2,16,2560]{4,3,2,1,0:T(8,128)(2,1)S(1)} collective-permute-done((bf16[2,4,2,16,2560]{4,3,2,1,0:T(8,128)(2,1)}, bf16[2,4,2,16,2560]{4,3,2,1,0:T(8,128)(2,1)S(1)}, u32[]{:S(2)}, u32[]{:S(2)}) %collective-permute-start) | collective-permute-done | bytes 1310752 | tf_op jit(solution)/shard_map/ppermute | solution.py:17
  58.1 1.8 maximum_maximum_fusion
  59.8 6.6 %collective-permute-start.1 = (bf16[2,8,2,16,2560]{4,3,2,1,0:T(8,128)(2,1)}, bf16[2,8,2,16,2560]{4,3,2,1,0:T(8,128)(2,1)}, u32[]{:S(2)}, u32[]{:S(2)}) collective-permute-start(bf16[2,8,2,16,2560]{4,3,2,1,0:T(8,128)(2,1)} %maximum_maximum_fusion), channel_id=1, source_target_pairs={{0,1},{1,2},{2,3},{3,4},{4,5},{5,6},{6,7},{8,9},{9,10},{10,11},{11... | collective-permute-start | bytes 7864328 | tf_op jit(solution)/shard_map/ppermute | solution.py:28
  66.4 1.9 collective-permute-start.2
  71.5 2.3 bitcast_reduce_fusion
  73.8 25.0 %collective-permute-done.1 = bf16[2,8,2,16,2560]{4,3,2,1,0:T(8,128)(2,1)} collective-permute-done((bf16[2,8,2,16,2560]{4,3,2,1,0:T(8,128)(2,1)}, bf16[2,8,2,16,2560]{4,3,2,1,0:T(8,128)(2,1)}, u32[]{:S(2)}, u32[]{:S(2)}) %collective-permute-start.1) | collective-permute-done | bytes 2621472 | tf_op jit(solution)/shard_map/ppermute | solution.py:28
  98.8 36.8 %collective-permute-done.2 = bf16[2,8,2,16,2560]{4,3,2,1,0:T(8,128)(2,1)} collective-permute-done((bf16[2,8,2,16,2560]{4,3,2,1,0:T(8,128)(2,1)}, bf16[2,8,2,16,2560]{4,3,2,1,0:T(8,128)(2,1)}, u32[]{:S(2)}, u32[]{:S(2)}) %collective-permute-start.2) | collective-permute-done | bytes 2621472 | tf_op jit(solution)/shard_map/ppermute | solution.py:30
  135.6 6.3 %pad_maximum_fusion.1 = bf16[2,8,6,16,2560]{4,3,2,1,0:T(8,128)(2,1)} fusion(bf16[2,8,2,16,2560]{4,3,2,1,0:T(8,128)(2,1)} %collective-permute-done.2, bf16[1,4,2,16,2560]{4,3,2,1,0:T(8,128)(2,1)S(1)} %bitcast.140, bf16[1,4,2,16,2560]{4,3,2,1,0:T(8,128)(2,1)S(1)} %bitcast.136, bf16[2,4,2,16,2560]{4,3,2,1,0:T(8,128)(2,1)S(1)} %collective-permute-done, ...), kind=kLoop, calls=%fused_computation.42 | loop fusion | flops 15728640 | bytes 15728640 | tf_op jit(solution)/shard_map/concatenate | solution.py:26
  143.1 73.8 %while.38 = (s32[]{:T(128)}, f32[20,128]{1,0:T(8,128)S(1)}, f32[20,128]{1,0:T(8,128)S(1)}, f32[128,20,128]{0,2,1:T(8,128)}, bf16[1,2,64,20,128]{4,2,3,1,0:T(8,12...) while((s32[]{:T(128)}, f32[20,128]{1,0:T(8,128)S(1)}, ...), condition=%wide.region_4.5_spmd.clone, body=%wide.region_1.4_spmd.clone.sunk | while | flops 321453056 | bytes 83591480 | solution.py:143
  146.9 2.5 fusion.45
  149.4 2.0 copy.118
  152.0 3.0 %fusion.46 = (f32[2,4,64]{2,1,0:T(4,128)S(1)}, f32[2,4,64,1152]{3,2,1,0:T(8,128)S(1)}) fusion(bf16[2,1152,4,128]{3,1,2,0:T(8,128)(2,1)} %bitcast.125, bf16[1,2,64,20,128]{4,2,3,1,0:T(8,128)(2,1)} %get-tuple-element.581, s32[]{:T(128)S(6)} %select_n.105, pred[2,64,1152]{2,1,0:T(8,128)(4,1)S(1)} %copy.119), kind=kOutput, calls=%fused_computation.77.clone.1 | convolution fusion | flops 152763904 | bytes 4999172 | tf_op jit(solution)/shard_map/while/body/eval_jaxpr/tcqhd,tckhd->tchqk/dot_general | solution.py:120
  161.6 2.5 fusion.45
  164.2 2.0 copy.118
  166.7 3.0 %fusion.46 = (f32[2,4,64]{2,1,0:T(4,128)S(1)}, f32[2,4,64,1152]{3,2,1,0:T(8,128)S(1)}) fusion(bf16[2,1152,4,128]{3,1,2,0:T(8,128)(2,1)} %bitcast.125, bf16[1,2,64,20,128]{4,2,3,1,0:T(8,128)(2,1)} %get-tuple-element.581, s32[]{:T(128)S(6)} %select_n.105, pred[2,64,1152]{2,1,0:T(8,128)(4,1)S(1)} %copy.119), kind=kOutput, calls=%fused_computation.77.clone.1 | convolution fusion | flops 152763904 | bytes 4999172 | tf_op jit(solution)/shard_map/while/body/eval_jaxpr/tcqhd,tckhd->tchqk/dot_general | solution.py:120
  176.4 2.5 fusion.45
  178.9 2.0 copy.118
  181.5 3.0 %fusion.46 = (f32[2,4,64]{2,1,0:T(4,128)S(1)}, f32[2,4,64,1152]{3,2,1,0:T(8,128)S(1)}) fusion(bf16[2,1152,4,128]{3,1,2,0:T(8,128)(2,1)} %bitcast.125, bf16[1,2,64,20,128]{4,2,3,1,0:T(8,128)(2,1)} %get-tuple-element.581, s32[]{:T(128)S(6)} %select_n.105, pred[2,64,1152]{2,1,0:T(8,128)(4,1)S(1)} %copy.119), kind=kOutput, calls=%fused_computation.77.clone.1 | convolution fusion | flops 152763904 | bytes 4999172 | tf_op jit(solution)/shard_map/while/body/eval_jaxpr/tcqhd,tckhd->tchqk/dot_general | solution.py:120
  191.2 2.5 fusion.45
  193.7 2.0 copy.118
  196.3 3.0 %fusion.46 = (f32[2,4,64]{2,1,0:T(4,128)S(1)}, f32[2,4,64,1152]{3,2,1,0:T(8,128)S(1)}) fusion(bf16[2,1152,4,128]{3,1,2,0:T(8,128)(2,1)} %bitcast.125, bf16[1,2,64,20,128]{4,2,3,1,0:T(8,128)(2,1)} %get-tuple-element.581, s32[]{:T(128)S(6)} %select_n.105, pred[2,64,1152]{2,1,0:T(8,128)(4,1)S(1)} %copy.119), kind=kOutput, calls=%fused_computation.77.clone.1 | convolution fusion | flops 152763904 | bytes 4999172 | tf_op jit(solution)/shard_map/while/body/eval_jaxpr/tcqhd,tckhd->tchqk/dot_general | solution.py:120
  205.9 2.5 fusion.45
  208.5 2.0 copy.118
  211.0 3.0 %fusion.46 = (f32[2,4,64]{2,1,0:T(4,128)S(1)}, f32[2,4,64,1152]{3,2,1,0:T(8,128)S(1)}) fusion(bf16[2,1152,4,128]{3,1,2,0:T(8,128)(2,1)} %bitcast.125, bf16[1,2,64,20,128]{4,2,3,1,0:T(8,128)(2,1)} %get-tuple-element.581, s32[]{:T(128)S(6)} %select_n.105, pred[2,64,1152]{2,1,0:T(8,128)(4,1)S(1)} %copy.119), kind=kOutput, calls=%fused_computation.77.clone.1 | convolution fusion | flops 152763904 | bytes 4999172 | tf_op jit(solution)/shard_map/while/body/eval_jaxpr/tcqhd,tckhd->tchqk/dot_general | solution.py:120
  216.9 37.5 %while.39 = (s32[]{:T(128)}, f32[20,128]{1,0:T(8,128)S(1)}, f32[20,128]{1,0:T(8,128)S(1)}, f32[128,20,128]{0,2,1:T(8,128)}, bf16[2,16,16,2560]{3,2,1,0:T(8,128)(...) while((s32[]{:T(128)}, f32[20,128]{1,0:T(8,128)S(1)}, ...), condition=%wide.region_9.10_spmd.clone, body=%wide.region_6.9_spmd.clone.sunk | while | flops 43929608 | bytes 16578803 | solution.py:176
  218.3 1.5 fusion.49
  222.9 1.5 fusion.49
  227.6 1.5 fusion.49
  232.3 1.5 fusion.49
  254.5 1.7 divide_convert_fusion
  (261 shorter events, 73.0 us)
Async XLA Ops:
  6.5 62.9 %copy-start = (bf16[4,2,16,2560]{3,2,1,0:T(8,128)(2,1)S(1)}, bf16[4,2,16,2560]{3,2,1,0:T(8,128)(2,1)}, u32[]{:S(2)}) copy-start(bf16[4,2,16,2560]{3,2,1,0:T(8,128)(2,1)} %param.9) | copy-start | bytes 1966084
  6.5 7.4 %copy-start.5 = (bf16[4,2,16,2560]{3,2,1,0:T(8,128)(2,1)S(1)}, bf16[4,2,16,2560]{3,2,1,0:T(8,128)(2,1)}, u32[]{:S(2)}) copy-start(bf16[4,2,16,2560]{3,2,1,0:T(8,128)(2,1)} %param.10) | copy-start | bytes 1966084
  6.5 7.4 %copy-start.6 = (bf16[4,2,16,2560]{3,2,1,0:T(8,128)(2,1)S(1)}, bf16[4,2,16,2560]{3,2,1,0:T(8,128)(2,1)}, u32[]{:S(2)}) copy-start(bf16[4,2,16,2560]{3,2,1,0:T(8,128)(2,1)} %param.11) | copy-start | bytes 1966084
  6.5 64.9 %all-gather.6.cloned.1.call-start = ((), (), s32[]{:S(2)}) async-start(), calls=%async_computation.1 | async-start | bytes 1638400 | tf_op jit(solution)/shard_map/all_gather | solution.py:39
  9.2 48.9 %collective-permute-start = (bf16[2,4,2,16,2560]{4,3,2,1,0:T(8,128)(2,1)}, bf16[2,4,2,16,2560]{4,3,2,1,0:T(8,128)(2,1)S(1)}, u32[]{:S(2)}, u32[]{:S(2)}) collective-permute-start(bf16[2,4,2,16,2560]{4,3,2,1,0:T(8,128)(2,1)} %pad_maximum_fusion.2), channel_id=1, source_target_pairs={{0,8},{8,16},{16,24},{1,9},{9,17},{17,25},{2,10},{10,18},{18,26},{... | collective-permute-start | bytes 3932168 | tf_op jit(solution)/shard_map/ppermute | solution.py:17
  14.8 53.8 %copy-start.8 = (s32[1,1,2,18]{3,2,1,0:T(2,128)S(1)}, s32[1,1,2,18]{3,2,1,0:T(2,128)}, u32[]{:S(2)}) copy-start(s32[1,1,2,18]{3,2,1,0:T(2,128)} %param.12) | copy-start | bytes 436
  14.8 202.2 %all-gather.4.cloned.1.call-start = ((), (), s32[]{:S(2)}) async-start(), calls=%async_computation | async-start | bytes 2949120 | tf_op jit(solution)/shard_map/all_gather | solution.py:153
  59.8 39.0 %collective-permute-start.1 = (bf16[2,8,2,16,2560]{4,3,2,1,0:T(8,128)(2,1)}, bf16[2,8,2,16,2560]{4,3,2,1,0:T(8,128)(2,1)}, u32[]{:S(2)}, u32[]{:S(2)}) collective-permute-start(bf16[2,8,2,16,2560]{4,3,2,1,0:T(8,128)(2,1)} %maximum_maximum_fusion), channel_id=1, source_target_pairs={{0,1},{1,2},{2,3},{3,4},{4,5},{5,6},{6,7},{8,9},{9,10},{10,11},{11... | collective-permute-start | bytes 7864328 | tf_op jit(solution)/shard_map/ppermute | solution.py:28
  66.4 69.2 %collective-permute-start.2 = (bf16[2,8,2,16,2560]{4,3,2,1,0:T(8,128)(2,1)}, bf16[2,8,2,16,2560]{4,3,2,1,0:T(8,128)(2,1)}, u32[]{:S(2)}, u32[]{:S(2)}) collective-permute-start(bf16[2,8,2,16,2560]{4,3,2,1,0:T(8,128)(2,1)} %maximum_maximum_fusion), channel_id=1, source_target_pairs={{1,0},{2,1},{3,2},{4,3},{5,4},{6,5},{7,6},{9,8},{10,9},{11,10},{12... | collective-permute-start | bytes 7864328 | tf_op jit(solution)/shard_map/ppermute | solution.py:30
  152.0 3.0 %copy-start.2 = (bf16[1,1,2,2,4,3,2,3,8,4,128]{10,8,9,2,7,6,5,4,3,1,0:T(8,128)(2,1)S(1)}, bf16[1,1,2,2,4,3,2,3,8,4,128]{10,8,9,2,7,6,5,4,3,1,0:T(8,128)(2,1)}, u32[]{:S(2)}) copy-start(bf16[1,1,2,2,4,3,2,3,8,4,128]{10,8,9,2,7,6,5,4,3,1,0:T(8,128)(2,1)} %get-tuple-element.501) | copy-start | bytes 7077892 | tf_op jit(solution)/shard_map/while
  166.7 3.0 %copy-start.2 = (bf16[1,1,2,2,4,3,2,3,8,4,128]{10,8,9,2,7,6,5,4,3,1,0:T(8,128)(2,1)S(1)}, bf16[1,1,2,2,4,3,2,3,8,4,128]{10,8,9,2,7,6,5,4,3,1,0:T(8,128)(2,1)}, u32[]{:S(2)}) copy-start(bf16[1,1,2,2,4,3,2,3,8,4,128]{10,8,9,2,7,6,5,4,3,1,0:T(8,128)(2,1)} %get-tuple-element.501) | copy-start | bytes 7077892 | tf_op jit(solution)/shard_map/while
  181.5 3.0 %copy-start.2 = (bf16[1,1,2,2,4,3,2,3,8,4,128]{10,8,9,2,7,6,5,4,3,1,0:T(8,128)(2,1)S(1)}, bf16[1,1,2,2,4,3,2,3,8,4,128]{10,8,9,2,7,6,5,4,3,1,0:T(8,128)(2,1)}, u32[]{:S(2)}) copy-start(bf16[1,1,2,2,4,3,2,3,8,4,128]{10,8,9,2,7,6,5,4,3,1,0:T(8,128)(2,1)} %get-tuple-element.501) | copy-start | bytes 7077892 | tf_op jit(solution)/shard_map/while
  196.3 3.0 %copy-start.2 = (bf16[1,1,2,2,4,3,2,3,8,4,128]{10,8,9,2,7,6,5,4,3,1,0:T(8,128)(2,1)S(1)}, bf16[1,1,2,2,4,3,2,3,8,4,128]{10,8,9,2,7,6,5,4,3,1,0:T(8,128)(2,1)}, u32[]{:S(2)}) copy-start(bf16[1,1,2,2,4,3,2,3,8,4,128]{10,8,9,2,7,6,5,4,3,1,0:T(8,128)(2,1)} %get-tuple-element.501) | copy-start | bytes 7077892 | tf_op jit(solution)/shard_map/while
  211.0 3.0 %copy-start.2 = (bf16[1,1,2,2,4,3,2,3,8,4,128]{10,8,9,2,7,6,5,4,3,1,0:T(8,128)(2,1)S(1)}, bf16[1,1,2,2,4,3,2,3,8,4,128]{10,8,9,2,7,6,5,4,3,1,0:T(8,128)(2,1)}, u32[]{:S(2)}) copy-start(bf16[1,1,2,2,4,3,2,3,8,4,128]{10,8,9,2,7,6,5,4,3,1,0:T(8,128)(2,1)} %get-tuple-element.501) | copy-start | bytes 7077892 | tf_op jit(solution)/shard_map/while
  216.9 37.5 %copy-start.7 = (f32[128,20,128]{0,2,1:T(8,128)S(1)}, f32[128,20,128]{0,2,1:T(8,128)}, u32[]{:S(2)}) copy-start(f32[128,20,128]{0,2,1:T(8,128)} %get-tuple-element.295) | copy-start | bytes 3932164
  217.0 3.1 %copy-start.3 = (f32[128,20,128]{0,2,1:T(8,128)S(1)}, f32[128,20,128]{0,2,1:T(8,128)}, u32[]{:S(2)}) copy-start(f32[128,20,128]{0,2,1:T(8,128)} %get-tuple-element.530) | copy-start | bytes 3932164 | tf_op jit(solution)/shard_map/while
  220.6 1.1 copy-start.4
  221.7 3.0 %copy-start.3 = (f32[128,20,128]{0,2,1:T(8,128)S(1)}, f32[128,20,128]{0,2,1:T(8,128)}, u32[]{:S(2)}) copy-start(f32[128,20,128]{0,2,1:T(8,128)} %get-tuple-element.530) | copy-start | bytes 3932164 | tf_op jit(solution)/shard_map/while
  225.3 1.1 copy-start.4
  226.4 3.0 %copy-start.3 = (f32[128,20,128]{0,2,1:T(8,128)S(1)}, f32[128,20,128]{0,2,1:T(8,128)}, u32[]{:S(2)}) copy-start(f32[128,20,128]{0,2,1:T(8,128)} %get-tuple-element.530) | copy-start | bytes 3932164 | tf_op jit(solution)/shard_map/while
  230.0 1.1 copy-start.4
  231.0 3.0 %copy-start.3 = (f32[128,20,128]{0,2,1:T(8,128)S(1)}, f32[128,20,128]{0,2,1:T(8,128)}, u32[]{:S(2)}) copy-start(f32[128,20,128]{0,2,1:T(8,128)} %get-tuple-element.530) | copy-start | bytes 3932164 | tf_op jit(solution)/shard_map/while
  234.6 1.1 copy-start.4
  235.7 3.0 %copy-start.3 = (f32[128,20,128]{0,2,1:T(8,128)S(1)}, f32[128,20,128]{0,2,1:T(8,128)}, u32[]{:S(2)}) copy-start(f32[128,20,128]{0,2,1:T(8,128)} %get-tuple-element.530) | copy-start | bytes 3932164 | tf_op jit(solution)/shard_map/while
  239.3 1.1 copy-start.4
  240.4 3.0 %copy-start.3 = (f32[128,20,128]{0,2,1:T(8,128)S(1)}, f32[128,20,128]{0,2,1:T(8,128)}, u32[]{:S(2)}) copy-start(f32[128,20,128]{0,2,1:T(8,128)} %get-tuple-element.530) | copy-start | bytes 3932164 | tf_op jit(solution)/shard_map/while
  244.0 1.1 copy-start.4
  245.1 3.0 %copy-start.3 = (f32[128,20,128]{0,2,1:T(8,128)S(1)}, f32[128,20,128]{0,2,1:T(8,128)}, u32[]{:S(2)}) copy-start(f32[128,20,128]{0,2,1:T(8,128)} %get-tuple-element.530) | copy-start | bytes 3932164 | tf_op jit(solution)/shard_map/while
  248.7 1.1 copy-start.4
  249.8 3.0 %copy-start.3 = (f32[128,20,128]{0,2,1:T(8,128)S(1)}, f32[128,20,128]{0,2,1:T(8,128)}, u32[]{:S(2)}) copy-start(f32[128,20,128]{0,2,1:T(8,128)} %get-tuple-element.530) | copy-start | bytes 3932164 | tf_op jit(solution)/shard_map/while
  253.4 1.1 copy-start.4
  254.5 3.4 %copy-start.1 = (bf16[4,2,16,2560]{3,2,1,0:T(8,128)(2,1)S(1)}, bf16[4,2,16,2560]{3,2,1,0:T(8,128)(2,1)}, u32[]{:S(2)}) copy-start(bf16[4,2,16,2560]{3,2,1,0:T(8,128)(2,1)} %param.9) | copy-start | bytes 1966084
Sparse Core Ops, SparseCore 0:
  14.9 48.1 all-gather.5
  73.9 44.7 all-gather.3
